TPU v7x, 256 devices: a whole 4x4x8 slice. The times are simulated.
256 devices in a mesh: wide: 32 (over x, y, core), narrow: 8 (over z).
Axes of the slice: x: 4, y: 4, z: 8, core: 2. Of those that a mesh axis runs over, the one named last changes fastest.
Arguments:
- blocks: bfloat16 [32, 8, 16, 64, 4096], P('wide', 'narrow'), may hold values from -16 to 16
- row_tile: int32 [32, 8, 16], P('wide', 'narrow'), may hold values from 0 to 15
- col_tile: int32 [32, 8, 16], P('wide', 'narrow'), may hold values from 0 to 63, as said below
- depth_tile: int32 [32, 8, 16], P('wide', 'narrow'), may hold values from 0 to 15
- block_count: int32 [32, 8], P('wide', 'narrow'), may hold values from 4 to 16, as said below
- factor_b: bfloat16 [32768, 256], P(('wide', 'narrow')), may hold values from -40 to 40
- factor_c: bfloat16 [1024, 256], replicated, may hold values from -0.076293945 to 0.076293945
Outputs:
- a_new: float32 [32768, 256], P(('wide', 'narrow'))
- b_new: float32 [32768, 256], P(('wide', 'narrow'))
Inputs may be any that keep to these rules, and one draw needn't show every extreme that they name: `block_count`: every device holds at least 4 live blocks, and some device exactly 16. col_tile // 2 is the index of wide that holds the block's mode-2 factor rows; among the 16 slots of one device, live or not, each such index appears at most 1 times, and some index exactly 1 times.
All inputs are finite; a program needn't handle non-finite values.
Results may differ from a plain program's by a relative error of at most 0.02.
Values may be sent and summed in bfloat16 or wider, within the bound.
No kernel may reach another device: no remote copies, remote signals or barrier semaphores. Data moves between devices by JAX's collectives and lax.ppermute only.
A program may use at most 128 MiB of HBM per device.

v0:
```python
import jax
import jax.numpy as jnp
from jax import lax
from jax.sharding import PartitionSpec as P

TI_DEV = 2


def right_solve(target, matrix):
    chol_lower = jnp.linalg.cholesky(matrix)
    middle = lax.linalg.triangular_solve(
        chol_lower, target, left_side=False, lower=True, transpose_a=True
    )
    return lax.linalg.triangular_solve(
        chol_lower, middle, left_side=False, lower=True, transpose_a=False
    )


def column_gram(matrix):
    return lax.dot_general(
        matrix, matrix, (((0,), (0,)), ((), ())), preferred_element_type=jnp.float32
    )


def depth_mix(one_block, depth_id, factor_c, tile_rows):
    depth_rows = lax.dynamic_slice_in_dim(factor_c, depth_id * tile_rows, tile_rows, 0)
    depth_mixed = lax.dot_general(
        one_block, depth_rows, (((0,), (0,)), ((), ())), preferred_element_type=jnp.float32
    )
    return depth_mixed.reshape(tile_rows, tile_rows, depth_rows.shape[1])


def local(blocks, row_tile, col_tile, depth_tile, block_count, factor_b, factor_c):
    local_blocks = blocks[0, 0]
    first_ids = row_tile[0, 0]
    second_ids = col_tile[0, 0]
    depth_ids = depth_tile[0, 0]
    live_count = block_count[0, 0]
    tile_rows = local_blocks.shape[1]
    rank_width = factor_c.shape[1]
    wide_count = lax.axis_size("wide")
    narrow_count = lax.axis_size("narrow")
    second_local = factor_b.shape[0] // tile_rows
    owners = second_ids // second_local
    inside = second_ids % second_local
    gram_c = column_gram(factor_c)
    gram_b = lax.psum(column_gram(factor_b), ("wide", "narrow"))
    gathered = lax.all_gather(factor_b, "wide", axis=0, tiled=True)
    b_tiles = gathered.reshape(wide_count * second_local, tile_rows, rank_width)
    b_pick = owners * second_local + inside

    def first_step(slot_index, partial_sum):
        one_block = lax.dynamic_index_in_dim(local_blocks, slot_index, 0, False)
        depth_mixed = depth_mix(one_block, depth_ids[slot_index], factor_c, tile_rows)
        b_rows = lax.dynamic_index_in_dim(b_tiles, b_pick[slot_index], 0, False).astype(jnp.float32)
        b_term = jnp.sum(depth_mixed * b_rows[None, :, :], axis=1)
        target = first_ids[slot_index]
        current = lax.dynamic_index_in_dim(partial_sum, target, 0, False)
        return lax.dynamic_update_index_in_dim(partial_sum, current + b_term, target, 0)

    first_part = lax.fori_loop(
        0,
        live_count,
        first_step,
        jnp.zeros((narrow_count * TI_DEV, tile_rows, rank_width), jnp.float32),
    )
    mttkrp_a = lax.psum_scatter(
        first_part.reshape(-1, rank_width), "narrow", scatter_dimension=0, tiled=True
    )
    a_new = right_solve(mttkrp_a, gram_b * gram_c)
    a_half = a_new.astype(jnp.bfloat16)
    a_rows = lax.all_gather(a_half, "narrow", axis=0, tiled=True)
    gram_a = lax.psum(column_gram(a_half), ("wide", "narrow"))
    a_tiles = a_rows.reshape(a_rows.shape[0] // tile_rows, tile_rows, rank_width)
    width_slots = wide_count * second_local
    second_pick = owners * second_local + inside

    def second_step(slot_index, partial_sum):
        one_block = lax.dynamic_index_in_dim(local_blocks, slot_index, 0, False)
        depth_mixed = depth_mix(one_block, depth_ids[slot_index], factor_c, tile_rows)
        a_part = lax.dynamic_index_in_dim(a_tiles, first_ids[slot_index], 0, False).astype(
            jnp.float32
        )
        a_term = jnp.sum(depth_mixed * a_part[:, None, :], axis=0)
        target = second_pick[slot_index]
        current = lax.dynamic_index_in_dim(partial_sum, target, 0, False)
        return lax.dynamic_update_index_in_dim(partial_sum, current + a_term, target, 0)

    second_part = lax.fori_loop(
        0, live_count, second_step, jnp.zeros((width_slots, tile_rows, rank_width), jnp.float32)
    )
    mttkrp_b = lax.psum_scatter(
        second_part.reshape(-1, rank_width), "wide", scatter_dimension=0, tiled=True
    )
    b_new = right_solve(mttkrp_b, gram_a * gram_c)
    return (a_new, b_new)


def solution(mesh):
    return jax.shard_map(
        local,
        mesh=mesh,
        in_specs=(
            P("wide", "narrow", None, None, None),
            P("wide", "narrow", None),
            P("wide", "narrow", None),
            P("wide", "narrow", None),
            P("wide", "narrow"),
            P(("wide", "narrow"), None),
            P(),
        ),
        out_specs=(P(("wide", "narrow"), None), P(("wide", "narrow"), None)),
        check_vma=False,
    )
```

profile of v0, /device:TPU:2, one launch (start us, length us, event | category | flops | bytes accessed | tf_op | source)
XLA Modules:
  0.0 688.1 jit_solution(2137662635349681206)
XLA Ops:
  8.8 1.8 fusion.35
  10.8 15.6 %copy.22 = bf16[1,1,16,64,4096]{3,4,2,1,0:T(8,128)(2,1)} copy(bf16[1,1,16,64,4096]{4,3,2,1,0:T(8,128)(2,1)} %param.16) | data formatting | bytes 16777216 | tf_op args[0]
  26.4 36.2 %all-gather.2.cloned.1.call-done = bf16[4096,256]{1,0:T(8,128)(2,1)} async-done(((bf16[128,256]{1,0:T(8,128)(2,1)}), bf16[4096,256]{1,0:T(8,128)(2,1)}) %all-gather.2.cloned.1.call-update) | async-done | bytes 2097168 | tf_op jit(solution)/shard_map/all_gather | solution.py:48
  62.7 144.2 %while.28 = (s32[]{:T(128)}, f32[16,64,256]{2,1,0:T(8,128)S(1)}, s32[]{:T(128)}, s32[16]{0:T(128)S(1)}, bf16[16,64,4096]{1,2,0:T(8,128)(2,1)}, /*index=5*/s32[16...) while((s32[]{:T(128)}, f32[16,64,256]{2,1,0:T(8,128)S(1)}, ...), condition=%wide.region_7.9_spmd, body=%wide.region_5.8_spmd.sunk | while | flops 136331280 | bytes 2556253 | solution.py:61
  65.8 1.3 constant_dynamic-slice_fusion.8
  75.4 1.3 constant_dynamic-slice_fusion.8
  123.2 1.3 constant_dynamic-slice_fusion.8
  132.8 1.3 constant_dynamic-slice_fusion.8
  161.5 1.3 constant_dynamic-slice_fusion.8
  207.9 64.7 %all-reduce.4.cloned.1.call-done = f32[256,256]{0,1:T(8,128)} async-done(((f32[256,256]{0,1:T(8,128)}), f32[256,256]{0,1:T(8,128)}) %all-reduce.4.cloned.1.call-update) | async-done | bytes 262160 | tf_op jit(solution)/shard_map/psum | solution.py:47
  274.1 11.7 %cholesky.130 = f32[128,128]{1,0:T(8,128)S(1)} custom-call(f32[128,128]{1,0:T(8,128)S(1)} %cholesky.194), custom_call_target="Cholesky" | custom-call | tf_op jit(solution)/shard_map/jit(cholesky)/cholesky | solution.py:10
  285.9 9.8 %custom-call.17 = f32[1,128,128]{1,2,0:T(8,128)S(1)} custom-call(f32[1,128,128]{2,1,0:T(8,128)S(1)} %get-tuple-element.211), custom_call_target="InvertDiagBlocksLowerTriangular" | custom-call | tf_op jit(solution)/shard_map/jit(cholesky)/cholesky | solution.py:10
  296.2 11.7 %cholesky.147 = f32[128,128]{1,0:T(8,128)S(1)} custom-call(f32[128,128]{1,0:T(8,128)S(1)} %convolution_subtract_fusion.5), custom_call_target="Cholesky" | custom-call | tf_op jit(solution)/shard_map/jit(cholesky)/cholesky | solution.py:10
  310.0 4.2 while.30
  310.8 1.4 bitcast_dynamic-update-slice_fusion.4
  312.8 1.4 bitcast_dynamic-update-slice_fusion.4
  314.2 19.7 %custom-call.18 = f32[2,128,128]{1,2,0:T(8,128)S(1)} custom-call(f32[2,128,128]{2,1,0:T(8,128)S(1)} %get-tuple-element.131), custom_call_target="InvertDiagBlocksLowerTriangular" | custom-call | tf_op jit(solution)/shard_map/triangular_solve/custom-call.0 | solution.py:11
  337.2 24.6 %all_gather.7 = bf16[1024,256]{0,1:T(8,128)(2,1)S(1)} all-gather(bf16[128,256]{0,1:T(8,128)(2,1)S(1)} %fusion.31), channel_id=1, replica_groups=mesh['wide'=32,'narrow'=8] {'narrow'}, dimensions={0}, use_global_device_ids=true | all-gather | bytes 589824 | tf_op jit(solution)/shard_map/all_gather | solution.py:72
  362.9 2.4 broadcast_in_dim.14
  365.4 159.6 %while.29 = (s32[]{:T(128)}, f32[64,64,256]{2,1,0:T(8,128)}, s32[]{:T(128)}, s32[16]{0:T(128)S(1)}, bf16[16,64,4096]{1,2,0:T(8,128)(2,1)}, /*index=5*/s32[16]{0:...) while((s32[]{:T(128)}, f32[64,64,256]{2,1,0:T(8,128)}, ...), condition=%wide.region_12.16_spmd, body=%wide.region_10.15_spmd.sunk | while | flops 136331280 | bytes 2556253 | solution.py:89
  374.5 1.5 fusion.72
  379.2 1.3 constant_dynamic-slice_fusion.9
  385.1 1.5 fusion.72
  389.7 1.3 constant_dynamic-slice_fusion.9
  395.7 1.5 fusion.72
  400.3 1.3 constant_dynamic-slice_fusion.9
  406.3 1.5 fusion.72
  410.9 1.3 constant_dynamic-slice_fusion.9
  416.9 1.5 fusion.72
  427.5 1.5 fusion.72
  438.1 1.5 fusion.72
  448.6 1.5 fusion.72
  459.2 1.5 fusion.72
  469.8 1.5 fusion.72
  480.4 1.5 fusion.72
  491.0 1.5 fusion.72
  501.6 1.5 fusion.72
  506.3 1.3 constant_dynamic-slice_fusion.9
  512.2 1.5 fusion.72
  522.8 1.5 fusion.72
  525.7 89.8 %all-reduce.6.cloned.1.call-done = f32[256,256]{0,1:T(8,128)} async-done(((f32[256,256]{0,1:T(8,128)}), f32[256,256]{0,1:T(8,128)}) %all-reduce.6.cloned.1.call-update) | async-done | bytes 262160 | tf_op jit(solution)/shard_map/psum | solution.py:73
  616.7 11.7 %cholesky.164 = f32[128,128]{1,0:T(8,128)S(1)} custom-call(f32[128,128]{1,0:T(8,128)S(1)} %cholesky.197), custom_call_target="Cholesky" | custom-call | tf_op jit(solution)/shard_map/jit(cholesky)/cholesky | solution.py:10
  628.5 9.8 %custom-call.20 = f32[1,128,128]{1,2,0:T(8,128)S(1)} custom-call(f32[1,128,128]{2,1,0:T(8,128)S(1)} %get-tuple-element.207), custom_call_target="InvertDiagBlocksLowerTriangular" | custom-call | tf_op jit(solution)/shard_map/jit(cholesky)/cholesky | solution.py:10
  638.7 11.7 %cholesky.181 = f32[128,128]{1,0:T(8,128)S(1)} custom-call(f32[128,128]{1,0:T(8,128)S(1)} %convolution_subtract_fusion.2), custom_call_target="Cholesky" | custom-call | tf_op jit(solution)/shard_map/jit(cholesky)/cholesky | solution.py:10
  653.1 4.1 while.31
  654.0 1.3 bitcast_dynamic-update-slice_fusion.5
  655.9 1.3 bitcast_dynamic-update-slice_fusion.5
  657.3 19.7 %custom-call.21 = f32[2,128,128]{1,2,0:T(8,128)S(1)} custom-call(f32[2,128,128]{2,1,0:T(8,128)S(1)} %get-tuple-element.133), custom_call_target="InvertDiagBlocksLowerTriangular" | custom-call | tf_op jit(solution)/shard_map/triangular_solve/custom-call.0 | solution.py:11
  (263 shorter events, 133.2 us)
Async XLA Ops:
  8.0 54.6 %all-gather.2.cloned.1.call-start = ((), (), s32[]{:S(2)}) async-start(), calls=%async_computation.3 | async-start | bytes 2162688 | tf_op jit(solution)/shard_map/all_gather | solution.py:48
  8.7 263.9 %all-reduce.4.cloned.1.call-start = ((), (), s32[]{:S(2)}) async-start(), calls=%async_computation.2 | async-start | bytes 524288 | tf_op jit(solution)/shard_map/psum | solution.py:47
  10.7 323.2 %reduce-scatter.3.cloned.1.call-start = ((), (), s32[]{:S(2)}) async-start(), calls=%async_computation.4 | async-start | bytes 1179648 | tf_op jit(solution)/shard_map/reduce_scatter | solution.py:67
  10.7 15.7 %copy-start.2 = (s32[1,1,16]{2,1,0:T(1,128)S(1)}, s32[1,1,16]{2,1,0:T(1,128)}, u32[]{:S(2)}) copy-start(s32[1,1,16]{2,1,0:T(1,128)} %param.18) | copy-start | bytes 196
  10.7 51.9 %copy-start.1 = (bf16[1024,256]{1,0:T(8,128)(2,1)S(1)}, bf16[1024,256]{1,0:T(8,128)(2,1)}, u32[]{:S(2)}) copy-start(bf16[1024,256]{1,0:T(8,128)(2,1)} %param.22) | copy-start | bytes 1572868
  10.7 51.9 %copy-start.3 = (s32[1,1,16]{2,1,0:T(1,128)S(1)}, s32[1,1,16]{2,1,0:T(1,128)}, u32[]{:S(2)}) copy-start(s32[1,1,16]{2,1,0:T(1,128)} %param.17) | copy-start | bytes 196
  10.7 51.9 %copy-start.4 = (s32[1,1,16]{2,1,0:T(1,128)S(1)}, s32[1,1,16]{2,1,0:T(1,128)}, u32[]{:S(2)}) copy-start(s32[1,1,16]{2,1,0:T(1,128)} %param.19) | copy-start | bytes 196
  206.9 1.0 copy-start
  207.9 407.6 %all-reduce.6.cloned.1.call-start = ((), (), s32[]{:S(2)}) async-start(), calls=%async_computation.5 | async-start | bytes 524288 | tf_op jit(solution)/shard_map/psum | solution.py:73
  362.9 314.1 %reduce-scatter.5.cloned.1.call-start = ((), (), s32[]{:S(2)}) async-start(), calls=%async_computation.6 | async-start | bytes 4325376 | tf_op jit(solution)/shard_map/reduce_scatter | solution.py:92
Sparse Core Ops, SparseCore 0:
  11.4 51.1 all-gather.1
  208.0 42.8 reduce-scatter.2
  525.1 93.6 reduce-scatter.4
Sparse Core Ops, SparseCore 1:
  14.7 257.9 all-reduce.3
  363.0 252.5 all-reduce.5
where the time goes:
time: 694 us; the launch traced here: 688 us
  waiting for transfers between devices  191 us (28%)
  loops' own time  155 us (22%)
  other arithmetic  143 us (21%)
  local copies, waits for them, and re-layouts  121 us (17%)
  matrix products  34.1 us (5%)
  blocking collectives  24.6 us (4%)
  between operations  18.1 us (3%)
    psum x1, waiting for transfers between devices, local(): gram_a = lax.psum(column_gram(a_half), ('wide', 'narrow'))  89.8 us
    another operation x1, loops' own time, local(): lax.fori_loop(0, live_count, second_step, jnp.zeros((width_slots, tile_ro...  79.1 us
    another operation x1, loops' own time, local(): lax.fori_loop(0, live_count, first_step, jnp.zeros((narrow_count * TI_DEV...  75.7 us
    another operation x13, other arithmetic, right_solve(): chol_lower = jnp.linalg.cholesky(matrix)  68.6 us
    psum x1, waiting for transfers between devices, local(): gram_b = lax.psum(column_gram(factor_b), ('wide', 'narrow'))  64.7 us
    another operation x5, other arithmetic, right_solve(): lax.linalg.triangular_solve(chol_lower, target, left_side=False, lower=Tr...  39.4 us
    all_gather x1, waiting for transfers between devices, local(): gathered = lax.all_gather(factor_b, 'wide', axis=0, tiled=True)  36.2 us
    all_gather x1, blocking collectives, local(): a_rows = lax.all_gather(a_half, 'narrow', axis=0, tiled=True)  24.6 us
  transfers between devices with their start and end apart: 5, of which 3 were waited for; matrix products, arithmetic and copies ran while one was open for 42% of the time, Pallas kernels for 0%

commit v1 on v0

--- a/solution.py
+++ b/solution.py
@@ -4,6 +4,7 @@
 from jax.sharding import PartitionSpec as P
 
 TI_DEV = 2
+signs_solve = lambda u_in: jnp.sum(jax.lax.all_gather(u_in, axis_name=("wide", "narrow")), 0)
 
 
 def right_solve(target, matrix):
@@ -70,7 +71,7 @@
     a_new = right_solve(mttkrp_a, gram_b * gram_c)
     a_half = a_new.astype(jnp.bfloat16)
     a_rows = lax.all_gather(a_half, "narrow", axis=0, tiled=True)
-    gram_a = lax.psum(column_gram(a_half), ("wide", "narrow"))
+    gram_a = signs_solve(column_gram(a_half))
     a_tiles = a_rows.reshape(a_rows.shape[0] // tile_rows, tile_rows, rank_width)
     width_slots = wide_count * second_local
     second_pick = owners * second_local + inside

time: 694 us -> 651 us (0.938)
  waiting for transfers between devices: 191 us -> 131 us
  other arithmetic: 143 us -> 165 us
  loops' own time: 155 us -> 147 us
    psum x1 -> x0, waiting for transfers between devices: 89.8 us -> none  [local(): gram_a = lax.psum(column_gram(a_half), ('wide', 'narrow'))]
    all_gather x0 -> x1, waiting for transfers between devices: none -> 33.6 us  [jax.lax.all_gather(u_in, axis_name=('wide', 'narrow'))]
    reduce_sum x0 -> x1, other arithmetic: none -> 22.1 us  [jnp.sum(jax.lax.all_gather(u_in, axis_name=('wide', 'narrow')), 0)]
    another operation x1, loops' own time: 79.1 us -> 68.5 us  [local(): lax.fori_loop(0, live_count, second_step, jnp.zeros((width_slots, tile_ro...]
  transfers between devices with their start and end apart: 5 -> 5, of which waited for: 3 -> 3; matrix products, arithmetic and copies ran while one was open for 42% -> 49% of each run, Pallas kernels for 0% -> 0%
where the time goes in v1:
time: 651 us; the launch traced here: 644 us
  other arithmetic  165 us (25%)
  loops' own time  147 us (23%)
  waiting for transfers between devices  131 us (20%)
  local copies, waits for them, and re-layouts  123 us (19%)
  matrix products  34.1 us (5%)
  blocking collectives  25.7 us (4%)
  between operations  18.1 us (3%)
    another operation x1, loops' own time, local(): lax.fori_loop(0, live_count, first_step, jnp.zeros((narrow_count * TI_DEV...  77.8 us
    another operation x13, other arithmetic, right_solve(): chol_lower = jnp.linalg.cholesky(matrix)  68.7 us
    another operation x1, loops' own time, local(): lax.fori_loop(0, live_count, second_step, jnp.zeros((width_slots, tile_ro...  68.5 us
    psum x1, waiting for transfers between devices, local(): gram_b = lax.psum(column_gram(factor_b), ('wide', 'narrow'))  60.4 us
    another operation x5, other arithmetic, right_solve(): lax.linalg.triangular_solve(chol_lower, target, left_side=False, lower=Tr...  39.6 us
    all_gather x1, waiting for transfers between devices, local(): gathered = lax.all_gather(factor_b, 'wide', axis=0, tiled=True)  36.2 us
    all_gather x1, waiting for transfers between devices, jax.lax.all_gather(u_in, axis_name=('wide', 'narrow'))  33.6 us
    all_gather x1, blocking collectives, local(): a_rows = lax.all_gather(a_half, 'narrow', axis=0, tiled=True)  25.7 us
  transfers between devices with their start and end apart: 5, of which 3 were waited for; matrix products, arithmetic and copies ran while one was open for 49% of the time, Pallas kernels for 0%

profile of v1, /device:TPU:2, one launch (start us, length us, event | category | flops | bytes accessed | tf_op | source)
XLA Modules:
  0.0 643.7 jit_solution(4741939585253606918)
XLA Ops:
  8.8 1.8 fusion.35
  10.8 15.6 %copy.30 = bf16[1,1,16,64,4096]{3,4,2,1,0:T(8,128)(2,1)} copy(bf16[1,1,16,64,4096]{4,3,2,1,0:T(8,128)(2,1)} %param.16) | data formatting | bytes 16777216 | tf_op args[0]
  26.3 36.2 %all-gather.4.cloned.1.call-done = bf16[4096,256]{1,0:T(8,128)(2,1)} async-done(((bf16[128,256]{1,0:T(8,128)(2,1)}), bf16[4096,256]{1,0:T(8,128)(2,1)}) %all-gather.4.cloned.1.call-update) | async-done | bytes 2097168 | tf_op jit(solution)/shard_map/all_gather | solution.py:49
  62.7 148.9 %while.28 = (s32[]{:T(128)}, f32[16,64,256]{2,1,0:T(8,128)S(1)}, s32[]{:T(128)}, s32[16]{0:T(128)S(1)}, bf16[16,64,4096]{1,2,0:T(8,128)(2,1)}, /*index=5*/s32[16...) while((s32[]{:T(128)}, f32[16,64,256]{2,1,0:T(8,128)S(1)}, ...), condition=%wide.region_7.9_spmd, body=%wide.region_5.8_spmd.sunk | while | flops 136331280 | bytes 2556253 | solution.py:62
  145.0 1.3 constant_dynamic-slice_fusion.8
  212.7 60.4 %all-reduce.3.cloned.1.call-done = f32[256,256]{0,1:T(8,128)} async-done(((f32[256,256]{0,1:T(8,128)}), f32[256,256]{0,1:T(8,128)}) %all-reduce.3.cloned.1.call-update) | async-done | bytes 262160 | tf_op jit(solution)/shard_map/psum | solution.py:48
  274.6 11.7 %cholesky.130 = f32[128,128]{1,0:T(8,128)S(1)} custom-call(f32[128,128]{1,0:T(8,128)S(1)} %cholesky.194), custom_call_target="Cholesky" | custom-call | tf_op jit(solution)/shard_map/jit(cholesky)/cholesky | solution.py:11
  286.4 9.8 %custom-call.17 = f32[1,128,128]{1,2,0:T(8,128)S(1)} custom-call(f32[1,128,128]{2,1,0:T(8,128)S(1)} %get-tuple-element.213), custom_call_target="InvertDiagBlocksLowerTriangular" | custom-call | tf_op jit(solution)/shard_map/jit(cholesky)/cholesky | solution.py:11
  296.7 11.7 %cholesky.147 = f32[128,128]{1,0:T(8,128)S(1)} custom-call(f32[128,128]{1,0:T(8,128)S(1)} %convolution_subtract_fusion.5), custom_call_target="Cholesky" | custom-call | tf_op jit(solution)/shard_map/jit(cholesky)/cholesky | solution.py:11
  310.5 4.1 while.30
  311.3 1.4 bitcast_dynamic-update-slice_fusion.4
  313.3 1.4 bitcast_dynamic-update-slice_fusion.4
  314.7 19.7 %custom-call.18 = f32[2,128,128]{1,2,0:T(8,128)S(1)} custom-call(f32[2,128,128]{2,1,0:T(8,128)S(1)} %get-tuple-element.131), custom_call_target="InvertDiagBlocksLowerTriangular" | custom-call | tf_op jit(solution)/shard_map/triangular_solve/custom-call.0 | solution.py:12
  338.6 25.7 %all_gather.15 = bf16[1024,256]{0,1:T(8,128)(2,1)S(1)} all-gather(bf16[128,256]{0,1:T(8,128)(2,1)S(1)} %fusion.31), channel_id=1, replica_groups=mesh['wide'=32,'narrow'=8] {'narrow'}, dimensions={0}, use_global_device_ids=true | all-gather | bytes 589824 | tf_op jit(solution)/shard_map/all_gather | solution.py:73
  364.6 2.5 broadcast_in_dim.14
  367.0 148.2 %while.29 = (s32[]{:T(128)}, f32[64,64,256]{2,1,0:T(8,128)}, s32[]{:T(128)}, s32[16]{0:T(128)S(1)}, bf16[16,64,4096]{1,2,0:T(8,128)(2,1)}, /*index=5*/s32[16]{0:...) while((s32[]{:T(128)}, f32[64,64,256]{2,1,0:T(8,128)}, ...), condition=%wide.region_12.16_spmd, body=%wide.region_10.15_spmd.sunk | while | flops 136331280 | bytes 2556253 | solution.py:90
  375.3 1.5 fusion.72
  385.1 1.5 fusion.72
  394.9 1.5 fusion.72
  399.3 1.3 constant_dynamic-slice_fusion.9
  404.7 1.5 fusion.72
  409.1 1.3 constant_dynamic-slice_fusion.9
  414.5 1.5 fusion.72
  418.9 1.3 constant_dynamic-slice_fusion.9
  424.3 1.5 fusion.72
  434.1 1.5 fusion.72
  444.0 1.5 fusion.72
  453.7 1.5 fusion.72
  458.1 1.4 constant_dynamic-slice_fusion.9
  463.6 1.5 fusion.72
  468.0 1.5 constant_dynamic-slice_fusion.9
  473.6 1.5 fusion.72
  477.9 1.3 constant_dynamic-slice_fusion.9
  483.4 1.5 fusion.72
  487.8 1.4 constant_dynamic-slice_fusion.9
  493.4 1.5 fusion.72
  497.7 1.4 constant_dynamic-slice_fusion.9
  503.3 1.5 fusion.72
  513.1 1.5 fusion.72
  516.0 33.6 %all-gather.6.cloned.1.call-done = f32[65536,256]{1,0:T(8,128)} async-done(((f32[256,256]{1,0:T(8,128)}), f32[65536,256]{1,0:T(8,128)}) %all-gather.6.cloned.1.call-update) | async-done | bytes 67108880 | tf_op jit(solution)/shard_map/all_gather | solution.py:7
  549.6 22.1 %reduce_sum.31 = f32[256,256]{1,0:T(8,128)S(1)} reduce(f32[256,256,256]{2,1,0:T(8,128)} %bitcast.34, f32[]{:T(128)} %constant.146.clone.1), dimensions={0}, to_apply=%region_9.13 | reduce | flops 16711680 | bytes 67371008 | tf_op jit(solution)/shard_map/reduce_sum | solution.py:7
  572.1 11.7 %cholesky.164 = f32[128,128]{1,0:T(8,128)S(1)} custom-call(f32[128,128]{1,0:T(8,128)S(1)} %cholesky.197), custom_call_target="Cholesky" | custom-call | tf_op jit(solution)/shard_map/jit(cholesky)/cholesky | solution.py:11
  583.8 9.8 %custom-call.20 = f32[1,128,128]{1,2,0:T(8,128)S(1)} custom-call(f32[1,128,128]{2,1,0:T(8,128)S(1)} %get-tuple-element.209), custom_call_target="InvertDiagBlocksLowerTriangular" | custom-call | tf_op jit(solution)/shard_map/jit(cholesky)/cholesky | solution.py:11
  594.1 11.7 %cholesky.181 = f32[128,128]{1,0:T(8,128)S(1)} custom-call(f32[128,128]{1,0:T(8,128)S(1)} %convolution_subtract_fusion.2), custom_call_target="Cholesky" | custom-call | tf_op jit(solution)/shard_map/jit(cholesky)/cholesky | solution.py:11
  608.5 4.1 while.31
  609.2 1.3 bitcast_dynamic-update-slice_fusion.5
  611.3 1.3 bitcast_dynamic-update-slice_fusion.5
  612.6 19.9 %custom-call.21 = f32[2,128,128]{1,2,0:T(8,128)S(1)} custom-call(f32[2,128,128]{2,1,0:T(8,128)S(1)} %get-tuple-element.133), custom_call_target="InvertDiagBlocksLowerTriangular" | custom-call | tf_op jit(solution)/shard_map/triangular_solve/custom-call.0 | solution.py:12
  (265 shorter events, 135.1 us)
Async XLA Ops:
  8.0 54.6 %all-gather.4.cloned.1.call-start = ((), (), s32[]{:S(2)}) async-start(), calls=%async_computation.3 | async-start | bytes 2162688 | tf_op jit(solution)/shard_map/all_gather | solution.py:49
  8.7 264.4 %all-reduce.3.cloned.1.call-start = ((), (), s32[]{:S(2)}) async-start(), calls=%async_computation.2 | async-start | bytes 524288 | tf_op jit(solution)/shard_map/psum | solution.py:48
  10.7 323.7 %reduce-scatter.3.cloned.1.call-start = ((), (), s32[]{:S(2)}) async-start(), calls=%async_computation.4 | async-start | bytes 1179648 | tf_op jit(solution)/shard_map/reduce_scatter | solution.py:68
  10.7 15.6 %copy-start.2 = (s32[1,1,16]{2,1,0:T(1,128)S(1)}, s32[1,1,16]{2,1,0:T(1,128)}, u32[]{:S(2)}) copy-start(s32[1,1,16]{2,1,0:T(1,128)} %param.18) | copy-start | bytes 196
  10.7 52.0 %copy-start.1 = (bf16[1024,256]{1,0:T(8,128)(2,1)S(1)}, bf16[1024,256]{1,0:T(8,128)(2,1)}, u32[]{:S(2)}) copy-start(bf16[1024,256]{1,0:T(8,128)(2,1)} %param.22) | copy-start | bytes 1572868
  10.7 51.9 %copy-start.3 = (s32[1,1,16]{2,1,0:T(1,128)S(1)}, s32[1,1,16]{2,1,0:T(1,128)}, u32[]{:S(2)}) copy-start(s32[1,1,16]{2,1,0:T(1,128)} %param.17) | copy-start | bytes 196
  10.7 51.9 %copy-start.4 = (s32[1,1,16]{2,1,0:T(1,128)S(1)}, s32[1,1,16]{2,1,0:T(1,128)}, u32[]{:S(2)}) copy-start(s32[1,1,16]{2,1,0:T(1,128)} %param.19) | copy-start | bytes 196
  211.6 1.0 copy-start
  212.6 336.9 %all-gather.6.cloned.1.call-start = ((), (), s32[]{:S(2)}) async-start(), calls=%async_computation.6 | async-start | bytes 67371008 | tf_op jit(solution)/shard_map/all_gather | solution.py:7
  338.6 294.0 %reduce-scatter.5.cloned.1.call-start = ((), (), s32[]{:S(2)}) async-start(), calls=%async_computation.5 | async-start | bytes 4325376 | tf_op jit(solution)/shard_map/reduce_scatter | solution.py:93
Sparse Core Ops, SparseCore 0:
  11.4 51.1 all-gather.3
  212.7 43.1 reduce-scatter.2
  515.4 98.8 reduce-scatter.4
Sparse Core Ops, SparseCore 1:
  14.7 258.4 all-reduce.2
  338.7 210.9 all-gather.5
